TPU v7x, 128 devices: a whole 4x4x4 slice. The times are simulated.
128 devices in a mesh: seq: 8 (over y, x_hi), rep: 16 (over x_lo, z, core).
Axes of the slice: x: 4 (x_hi: 2, x_lo: 2; x = x_hi * 2 + x_lo), y: 4, z: 4, core: 2. Of those that a mesh axis runs over, the one named last changes fastest.
Arguments:
- tile_embed: bfloat16 [16, 8192, 768], P('rep', 'seq'), may hold values from -6 to 6
- tile_source: int32 [16, 8192], P('rep', 'seq'), may hold values from 0 to 8191, as said below
- slide_len: int32 [16], P('rep'), may hold values from 4096 to 8192
- grad_out: bfloat16 [16, 8192, 768], P('rep', 'seq'), may hold values from -6 to 6
- w_query: bfloat16 [768, 768], replicated, may hold values from -0.11727427342914273 to 0.11727427342914273
- w_key: bfloat16 [768, 768], replicated, may hold values from -0.11727427342914273 to 0.11727427342914273
- w_value: bfloat16 [768, 768], replicated, may hold values from -0.21875 to 0.21875
- w_out: bfloat16 [768, 768], replicated, may hold values from -0.21875 to 0.21875
Outputs:
- encoded: bfloat16 [16, 8192, 768], P('rep', 'seq')
- embed_grad: bfloat16 [16, 8192, 768], P('rep', 'seq')
- grad_query: float32 [768, 768], replicated
- grad_key: float32 [768, 768], replicated
- grad_value: float32 [768, 768], replicated
- grad_outproj: float32 [768, 768], replicated
Inputs may be any that keep to these rules, and one draw needn't show every extreme that they name: For each slide, tile_source is a permutation of 0 to 8191; each run of 1024 slide positions (aligned) takes exactly 1024 // (number of such runs) rows from each aligned run of 1024 rows of tile_embed.
All inputs are finite; a program needn't handle non-finite values.
Results may differ from a plain program's by a relative error of at most 0.0025.
The roundings to bfloat16 on the way count: a program that leaves them out, or rounds other values in their place, can miss the bound.
Values may be sent and summed in bfloat16 or wider, within the bound.
A program may use at most 192 MiB of HBM per device.

v0:
```python
import jax
import jax.numpy as jnp
from jax import lax
from jax.sharding import PartitionSpec as P

HEADS = 16
SEG = 1024
RATE = 16
NEGATIVE = -1e30


def sent_together(arrays, axis, dim, along):
    both = jnp.concatenate(arrays, axis=along)
    result, at, done = (lax.all_gather(both, axis, axis=dim, tiled=True), 0, [])
    for a in arrays:
        done.append(lax.slice_in_dim(result, at, at + a.shape[along], axis=along))
        at += a.shape[along]
    return tuple(done)


def side_by_side(arrays, axis, dim, along):
    widths = [a.shape[along] for a in arrays]
    both = jnp.concatenate(arrays, axis=along)
    result = lax.psum_scatter(both, axis, scatter_dimension=dim, tiled=True)
    return tuple(jnp.split(result, [sum(widths[:k]) for k in range(1, len(widths))], axis=along))


def chosen(dilation, head_count):
    return jnp.arange(dilation)[:, None] == (jnp.arange(head_count) % dilation)[None, :]


def sparse_rows(dense, dilation):
    row_count, head_count, trailing = dense.shape
    blocks = dense.astype(jnp.float32).reshape(
        row_count // dilation, dilation, head_count, trailing
    )
    selected = chosen(dilation, head_count)[None, :, :, None]
    return jnp.sum(jnp.where(selected, blocks, jnp.float32(0.0)), axis=1)


def spread_rows(sparse, dilation, filler):
    row_count, head_count, trailing = sparse.shape
    selected = chosen(dilation, head_count)[None, :, :, None]
    spread = jnp.where(selected, sparse[:, None], jnp.float32(filler))
    return spread.reshape(row_count * dilation, head_count, trailing)


def product(pattern, left_side, right_side):
    return jnp.einsum(pattern, left_side, right_side, preferred_element_type=jnp.float32)


def masked_scores(queries, key_rows, key_ok, pieces, scaling):
    scores = product("nqd,nkd->nqk", queries, key_rows) * scaling
    return jnp.where(key_ok.reshape(pieces, 1, -1), scores, NEGATIVE)


def head_forward(queries, key_rows, values, key_ok, pieces, scaling):
    head_width = queries.shape[-1]
    queries = queries.reshape(pieces, -1, head_width)
    key_rows = key_rows.reshape(pieces, -1, head_width)
    values = values.reshape(pieces, -1, head_width)
    scores = masked_scores(queries, key_rows, key_ok, pieces, scaling)
    maxima = jnp.max(scores, axis=-1)
    weights = jnp.exp(scores - maxima[..., None])
    totals = jnp.sum(weights, axis=-1)
    numerator = product("nqk,nkd->nqd", weights.astype(jnp.bfloat16), values)
    return (numerator.reshape(-1, head_width), maxima.reshape(-1), totals.reshape(-1))


def split_pieces(arrays, pieces):
    return tuple((member.reshape(pieces, -1, member.shape[-1]) for member in arrays))


def score_terms(queries, key_rows, values, key_ok, log_total, upstream, deltas, pieces, scaling):
    scores = masked_scores(queries, key_rows, key_ok, pieces, scaling)
    probabilities = jnp.exp(scores - log_total.reshape(pieces, -1, 1))
    prob_grad = product("nqd,nkd->nqk", upstream, values)
    score_grad = (probabilities * (prob_grad - deltas.reshape(pieces, -1, 1))).astype(jnp.bfloat16)
    return (probabilities, score_grad)


def head_backward(queries, key_rows, values, key_ok, log_total, upstream, deltas, pieces, scaling):
    head_width = queries.shape[-1]
    queries, key_rows, values, upstream = split_pieces(
        (queries, key_rows, values, upstream), pieces
    )
    probabilities, score_grad = score_terms(
        queries, key_rows, values, key_ok, log_total, upstream, deltas, pieces, scaling
    )
    value_grad = product("nqk,nqd->nkd", probabilities.astype(jnp.bfloat16), upstream)
    query_grad = product("nqk,nkd->nqd", score_grad, key_rows) * scaling
    key_grad = product("nqk,nqd->nkd", score_grad, queries) * scaling
    return (
        query_grad.reshape(-1, head_width),
        key_grad.reshape(-1, head_width),
        value_grad.reshape(-1, head_width),
    )


def heads_map(function, arrays, pieces, scaling):
    transposed = tuple((jnp.moveaxis(member, 1, 0) for member in arrays))
    results = lax.map(lambda members: function(*members, pieces, scaling), transposed)
    return tuple((jnp.moveaxis(member, 0, 1) for member in results))


def merge_parts(local_part, remote, dilation):
    numer_local, max_local, total_local = local_part
    numer_far = spread_rows(remote[0], dilation, 0.0)
    max_far = spread_rows(remote[1][..., None], dilation, NEGATIVE)[..., 0]
    total_far = spread_rows(remote[2][..., None], dilation, 0.0)[..., 0]
    highest = jnp.maximum(max_local, max_far)
    weight_local = jnp.exp(max_local - highest)
    weight_far = jnp.exp(max_far - highest)
    combined = total_local * weight_local + total_far * weight_far
    output = (numer_local * weight_local[..., None] + numer_far * weight_far[..., None]) / combined[
        ..., None
    ]
    return (output, highest + jnp.log(combined))


def project(left_side, right_side):
    return jnp.dot(left_side, right_side, preferred_element_type=jnp.float32)


def per_device(tile_embed, tile_source, slide_len, grad_out, w_query, w_key, w_value, w_out):
    owned_rows = tile_embed[0]
    source = tile_source[0]
    row_count, features = owned_rows.shape
    stripes = lax.axis_size("seq")
    stripe = lax.axis_index("seq")
    portion = row_count // stripes
    owner_dev = source // row_count
    ordering = jnp.argsort(owner_dev, stable=True)
    wanted = (source % row_count)[ordering].reshape(stripes, portion)
    requested = lax.all_to_all(wanted, "seq", split_axis=0, concat_axis=0, tiled=True)
    picked = jnp.take(owned_rows, requested.reshape(-1), axis=0).reshape(stripes, portion, features)
    arrived = lax.all_to_all(picked, "seq", split_axis=0, concat_axis=0, tiled=True).reshape(
        row_count, features
    )
    embedded = jnp.zeros_like(arrived).at[ordering].set(arrived)
    length = slide_len[0]
    upstream_in = grad_out[0]
    head_dim = features // HEADS
    scaling = head_dim ** (-0.5)
    positions = stripe * row_count + jnp.arange(row_count)
    valid_rows = positions < length
    queries = project(embedded, w_query).astype(jnp.bfloat16).reshape(row_count, HEADS, head_dim)
    key_rows = project(embedded, w_key).astype(jnp.bfloat16).reshape(row_count, HEADS, head_dim)
    values = project(embedded, w_value).astype(jnp.bfloat16).reshape(row_count, HEADS, head_dim)
    local_ok = jnp.broadcast_to(valid_rows[:, None], (row_count, HEADS))
    local_part = heads_map(
        head_forward, (queries, key_rows, values, local_ok), row_count // SEG, scaling
    )
    sparse_q = sparse_rows(queries, RATE).astype(jnp.bfloat16)
    sparse_k = sparse_rows(key_rows, RATE).astype(jnp.bfloat16)
    sparse_v = sparse_rows(values, RATE).astype(jnp.bfloat16)
    near_count = sparse_k.shape[0]
    far_k, far_v = sent_together(
        (sparse_k.reshape(near_count, features), sparse_v.reshape(near_count, features)),
        "seq",
        0,
        1,
    )
    far_count = far_k.shape[0]
    far_k = far_k.reshape(far_count, HEADS, head_dim)
    far_v = far_v.reshape(far_count, HEADS, head_dim)
    sparse_pos = jnp.arange(far_count)[:, None] * RATE + (jnp.arange(HEADS) % RATE)[None, :]
    sparse_ok = sparse_pos < length
    remote = heads_map(head_forward, (sparse_q, far_k, far_v, sparse_ok), 1, scaling)
    output, log_total = merge_parts(local_part, remote, RATE)
    attended = (
        (output * valid_rows[:, None, None]).astype(jnp.bfloat16).reshape(row_count, features)
    )
    encoded = (embedded.astype(jnp.float32) + project(attended, w_out)).astype(jnp.bfloat16)
    upstream = (
        (project(upstream_in, w_out.T) * valid_rows[:, None])
        .astype(jnp.bfloat16)
        .reshape(row_count, HEADS, head_dim)
    )
    deltas = jnp.sum(upstream.astype(jnp.float32) * output, axis=-1)
    grad_outproj = jnp.einsum(
        "td,te->de", attended, upstream_in, preferred_element_type=jnp.float32
    )
    local_grads = heads_map(
        head_backward,
        (queries, key_rows, values, local_ok, log_total, upstream, deltas),
        row_count // SEG,
        scaling,
    )
    sparse_up = sparse_rows(upstream, RATE).astype(jnp.bfloat16)
    sparse_delta = sparse_rows(deltas[..., None], RATE)[..., 0]
    sparse_total = sparse_rows(log_total[..., None], RATE)[..., 0]
    remote_grads = heads_map(
        head_backward,
        (sparse_q, far_k, far_v, sparse_ok, sparse_total, sparse_up, sparse_delta),
        1,
        scaling,
    )
    key_back, value_back = side_by_side(
        (
            remote_grads[1].reshape(far_count, features),
            remote_grads[2].reshape(far_count, features),
        ),
        "seq",
        0,
        1,
    )
    key_back = key_back.reshape(near_count, HEADS, head_dim)
    value_back = value_back.reshape(near_count, HEADS, head_dim)
    query_far = remote_grads[0]
    query_grad = (
        (local_grads[0] + spread_rows(query_far, RATE, 0.0))
        .astype(jnp.bfloat16)
        .reshape(row_count, features)
    )
    key_grad = (
        (local_grads[1] + spread_rows(key_back, RATE, 0.0))
        .astype(jnp.bfloat16)
        .reshape(row_count, features)
    )
    value_grad = (
        (local_grads[2] + spread_rows(value_back, RATE, 0.0))
        .astype(jnp.bfloat16)
        .reshape(row_count, features)
    )
    embed_grad = upstream_in.astype(jnp.float32) + project(query_grad, w_query.T)
    embed_grad = embed_grad + project(key_grad, w_key.T)
    embed_grad = (embed_grad + project(value_grad, w_value.T)).astype(jnp.bfloat16)
    grad_query = jnp.einsum("td,te->de", embedded, query_grad, preferred_element_type=jnp.float32)
    grad_key = jnp.einsum("td,te->de", embedded, key_grad, preferred_element_type=jnp.float32)
    grad_value = jnp.einsum("td,te->de", embedded, value_grad, preferred_element_type=jnp.float32)
    summed = lax.psum((grad_query, grad_key, grad_value, grad_outproj), ("seq", "rep"))
    return (encoded[None], embed_grad[None], summed[0], summed[1], summed[2], summed[3])


def solution(mesh):
    return jax.shard_map(
        per_device,
        mesh=mesh,
        in_specs=(
            P("rep", "seq", None),
            P("rep", "seq"),
            P("rep"),
            P("rep", "seq", None),
            P(),
            P(),
            P(),
            P(),
        ),
        out_specs=(P("rep", "seq", None), P("rep", "seq", None), P(), P(), P(), P()),
        check_vma=False,
    )
```

profile of v0, /device:TPU:1, one launch (start us, length us, event | category | flops | bytes accessed | tf_op | source)
XLA Modules:
  0.0 927.7 jit_solution(13894790200978015584)
XLA Ops:
  12.4 4.5 gather_fusion
  16.9 13.8 %all_to_all.14 = s32[8,1,128]{2,1,0:T(1,128)S(1)} all-to-all(s32[8,1,128]{2,1,0:T(1,128)S(1)} %bitcast.386), channel_id=1, replica_groups=mesh['seq'=8,'rep'=16] {'seq'}, dimensions={0} | all-to-all | bytes 8192 | tf_op jit(solution)/shard_map/all_to_all | solution.py:135
  47.3 4.8 copy.100
  55.3 7.8 reshape.434
  65.1 6.4 scatter_custom_fusion
  76.8 7.8 reshape.431
  90.0 7.8 reshape.432
  105.1 7.8 reshape.433
  112.9 14.1 %select_reduce_fusion = (bf16[64,16,48]{2,1,0:T(8,128)(2,1)S(1)}, bf16[64,16,48]{2,1,0:T(8,128)(2,1)}, bf16[64,16,48]{2,1,0:T(8,128)(2,1)}, bf16[64,16,48]{2,1,0:T(8,128)(2,1)}) fusion(f32[64,16,16,48]{3,2,1,0:T(8,128)} %reshape.434, pred[16,16]{1,0:T(8,128)(4,1)} %copy-done.23, f32[64,16,16,48]{3,2,1,0:T(8,128)} %reshape.432, ...), kind=kLoop, calls=%fused_computation.133 | loop fusion | flops 6094848 | bytes 12976384 | tf_op jit(solution)/shard_map/reduce_sum | solution.py:38
  144.3 142.6 %while.56 = (s32[]{:T(128)}, f32[16,1024,48]{1,2,0:T(8,128)}, f32[16,1024]{1,0:T(8,128)S(1)}, f32[16,1024]{1,0:T(8,128)S(1)}, pred[16,1024]{1,0:T(8,128)(4,1)S(1...) while((s32[]{:T(128)}, f32[16,1024,48]{1,2,0:T(8,128)}, ...), condition=%wide.region_5.6_spmd, body=%wide.region_2.5_spmd.sunk | while | flops 212858880 | bytes 30383244 | solution.py:102
  287.0 7.9 copy.83
  301.3 42.2 %while.57 = (s32[]{:T(128)}, f32[16,64,48]{1,2,0:T(8,128)S(1)}, f32[16,64]{1,0:T(8,128)S(1)}, f32[16,64]{1,0:T(8,128)S(1)}, pred[16,512]{1,0:T(8,128)(4,1)S(1)},...) while((s32[]{:T(128)}, f32[16,64,48]{1,2,0:T(8,128)S(1)}, ...), condition=%wide.region_12.13_spmd, body=%wide.region_9.12_spmd.sunk | while | flops 6520706 | bytes 702321 | solution.py:102
  346.2 13.4 %multiply_convert_fusion.1 = (bf16[1024,16,48]{2,1,0:T(8,128)(2,1)}, f32[1024,16,48]{2,1,0:T(8,128)S(1)}) fusion(f32[1024]{0:T(1024)S(1)} %copy-done.25, f32[1024,16]{1,0:T(8,128)} %copy.97, f32[1024,16]{1,0:T(8,128)S(1)} %copy.96, f32[64,16,48]{2,1,0:T(8,128)S(1)} %copy.95, pred[1024,16]{1,0:T(8,128)(4,1)S(1)} %copy.94, f32[1024,16]{1,0:T(8,128)S(1)} %copy.93, ...), kind=kLoop, calls=%fused_computation.135 | loop fusion | flops 5505024 | bytes 8278016 | tf_op jit(solution)/shard_map/convert_element_type | solution.py:172
  362.9 103.9 %while.59 = (s32[]{:T(128)}, f32[16,64,48]{1,2,0:T(8,128)S(1)}, f32[16,512,48]{1,2,0:T(8,128)}, f32[16,512,48]{1,2,0:T(8,128)}, pred[16,512]{1,0:T(8,128)(4,1)S(...) while((s32[]{:T(128)}, f32[16,64,48]{1,2,0:T(8,128)S(1)}, ...), condition=%wide.region_20.21_spmd, body=%wide.region_19.20_spmd.sunk | while | flops 15985666 | bytes 1278077 | solution.py:102
  481.0 181.1 %while.58 = (s32[]{:T(128)}, f32[16,1024,48]{1,2,0:T(8,128)}, f32[16,1024,48]{1,2,0:T(8,128)}, f32[16,1024,48]{1,2,0:T(8,128)}, pred[16,1024]{1,0:T(8,128)(4,1)S...) while((s32[]{:T(128)}, f32[16,1024,48]{1,2,0:T(8,128)}, ...), condition=%wide.region_15.16_spmd, body=%wide.region_14.15_spmd.sunk | while | flops 513900544 | bytes 21337212 | solution.py:102
  662.5 7.9 copy.102
  670.3 7.8 copy.112
  678.2 7.8 copy.115
  686.0 5.5 copy.98
  699.3 15.1 %fusion.110 = (bf16[1024,16,48]{2,1,0:T(8,128)(2,1)}, bf16[1024,16,48]{2,1,0:T(8,128)(2,1)}, bf16[1024,16,48]{2,1,0:T(8,128)(2,1)}) fusion(f32[16,1024,48]{2,0,1:T(8,128)} %copy.102, f32[64,16,48]{2,1,0:T(8,128)S(1)} %copy.110, pred[1024,16]{1,0:T(8,128)(4,1)} %copy-done.14, f32[64,16,48]{2,1,0:T(8,128)S(1)} %copy.113, f32[16,1024,48]{2,0,1:T(8,128)} %copy.112, ...), kind=kLoop, calls=%fused_computation.127 | loop fusion | flops 7077888 | bytes 14761984 | tf_op jit(solution)/shard_map/convert_element_type | solution.py:213
  714.4 5.5 copy.111
  724.2 5.5 copy.114
  742.7 5.0 fusion.117
  753.6 157.5 %all-reduce.3.cloned.1.call-done = (f32[768,768]{1,0:T(8,128)}, f32[768,768]{1,0:T(8,128)}, f32[768,768]{1,0:T(8,128)}, f32[768,768]{1,0:T(8,128)}) async-done(((f32[768,768]{1,0:T(8,128)}, f32[768,768]{1,0:T(8,128)}, f32[768,768]{1,0:T(8,128)}, f32[768,768]{1,0:T(8,128)}), (f32[768,768]{1,0:T(8,128)}, f32[768,768]{1,0:T(8,128)}, f32[768,768]{1,0:T(8,128)}, ...) | async-done | bytes 9437200 | tf_op jit(solution)/shard_map/psum | solution.py:232
  (605 shorter events, 596.5 us)
Async XLA Ops:
  7.2 23.6 %copy-start = (bf16[1,1024,768]{2,1,0:T(8,128)(2,1)S(1)}, bf16[1,1024,768]{2,1,0:T(8,128)(2,1)}, u32[]{:S(2)}) copy-start(bf16[1,1024,768]{2,1,0:T(8,128)(2,1)} %param.16) | copy-start | bytes 4718596
  36.1 6.4 copy-start.8
  36.1 29.0 %all-to-all-start.1 = ((bf16[8,128,768]{2,1,0:T(8,128)(2,1)}), bf16[8,128,768]{2,1,0:T(8,128)(2,1)}, u32[]{:S(2)}, u32[]{:S(2)}) async-start(bf16[8,128,768]{2,1,0:T(8,128)(2,1)} %broadcast_select_fusion), calls=%async_computation.1 | async-start | bytes 3145728 | tf_op jit(solution)/shard_map/all_to_all | solution.py:137
  40.5 255.1 %all-gather.2.cloned.1.call-start = ((), (), s32[]{:S(2)}) async-start(), calls=%async_computation.3 | async-start | bytes 1769472 | tf_op jit(solution)/shard_map/all_gather | solution.py:14
  64.4 281.8 %copy-start.14 = (pred[1024,16]{1,0:T(8,128)(4,1)}, pred[1024,16]{1,0:T(8,128)(4,1)S(1)}, u32[]{:S(2)}) copy-start(pred[1024,16]{1,0:T(8,128)(4,1)S(1)} %copy.94) | copy-start | bytes 49156
  71.5 3.3 copy-start.10
  132.4 563.3 %reduce-scatter.4.cloned.1.call-start = ((), (), s32[]{:S(2)}) async-start(), calls=%async_computation.4 | async-start | bytes 3538944
  135.9 3.2 copy-start.4
  139.0 3.2 copy-start.28
  139.0 5.3 copy-start.19
  139.0 5.3 copy-start.20
  144.3 142.7 %copy-start.16 = (bf16[64,16,48]{2,1,0:T(8,128)(2,1)S(1)}, bf16[64,16,48]{2,1,0:T(8,128)(2,1)}, u32[]{:S(2)}) copy-start(bf16[64,16,48]{2,1,0:T(8,128)(2,1)} %get-tuple-element.310) | copy-start | bytes 294916
  343.4 2.7 copy-start.25
  346.2 13.4 %copy-start.3 = (bf16[1024,16,48]{2,1,0:T(8,128)(2,1)S(1)}, bf16[1024,16,48]{2,1,0:T(8,128)(2,1)}, u32[]{:S(2)}) copy-start(bf16[1024,16,48]{2,1,0:T(8,128)(2,1)} %copy.100) | copy-start | bytes 4718596
  359.6 3.0 copy-start.22
  474.7 436.5 %all-reduce.3.cloned.1.call-start = ((), (), s32[]{:S(2)}) async-start(), calls=%async_computation.5 | async-start | bytes 18874368 | tf_op jit(solution)/shard_map/psum | solution.py:232
  686.0 5.5 copy-start.9
  714.4 5.5 copy-start.11
  742.7 5.0 copy-start.12
  742.7 5.0 copy-start.29
  911.1 3.4 copy-start.7
  914.5 2.5 copy-start.6
  917.0 2.5 copy-start.5
  917.0 3.9 copy-start.1
  (26 other events, 46.8 us)
Sparse Core Ops, SparseCore 0:
  132.6 52.8 all-gather.1
  474.8 81.6 reduce-scatter.3
  742.8 168.2 all-reduce.2
where the time goes:
time: 942 us; the launch traced here: 928 us
  matrix products  454 us (48%)
  local copies, waits for them, and re-layouts  204 us (22%)
  waiting for transfers between devices  158 us (17%)
  other arithmetic  76.5 us (8%)
  between operations  15.1 us (2%)
  blocking collectives  13.8 us (1%)
    dot_general x224, matrix products, product(): jnp.einsum(pattern, left_side, right_side, preferred_element_type=jnp.flo...  413 us
    psum x1, waiting for transfers between devices, per_device(): lax.psum((grad_query, grad_key, grad_value, grad_outproj), ('seq', 'rep'))  158 us
    while x9, local copies, waits for them, and re-layouts, heads_map(): lax.map(lambda members: function(*members, pieces, scaling), transposed)  35.9 us
    while x32, local copies, waits for them, and re-layouts  30.8 us
    convert_element_type x6, local copies, waits for them, and re-layouts, sparse_rows(): dense.astype(jnp.float32)  30.7 us
    dot_general x8, matrix products, project(): return jnp.dot(left_side, right_side, preferred_element_type=jnp.float32)  24 us
  transfers between devices with their start and end apart: 4, of which 1 were waited for; matrix products, arithmetic and copies ran while one was open for 41% of the time, Pallas kernels for 0%

commit v1 on v0

--- a/solution.py
+++ b/solution.py
@@ -1,3 +1,4 @@
+import functools
 import jax
 import jax.numpy as jnp
 from jax import lax
@@ -7,6 +8,13 @@
 SEG = 1024
 RATE = 16
 NEGATIVE = -1e30
+
+
+def supply_the_slots(unit, group_axis, bus_axis):
+    return lax.psum(lax.psum(unit, axis_name=group_axis), bus_axis)
+
+
+change_teams = functools.partial(supply_the_slots, group_axis="seq", bus_axis="rep")
 
 
 def sent_together(arrays, axis, dim, along):
@@ -229,7 +237,7 @@
     grad_query = jnp.einsum("td,te->de", embedded, query_grad, preferred_element_type=jnp.float32)
     grad_key = jnp.einsum("td,te->de", embedded, key_grad, preferred_element_type=jnp.float32)
     grad_value = jnp.einsum("td,te->de", embedded, value_grad, preferred_element_type=jnp.float32)
-    summed = lax.psum((grad_query, grad_key, grad_value, grad_outproj), ("seq", "rep"))
+    summed = change_teams((grad_query, grad_key, grad_value, grad_outproj))
     return (encoded[None], embed_grad[None], summed[0], summed[1], summed[2], summed[3])
 
 

time: 942 us -> 1310 us (1.39)
  waiting for transfers between devices: 158 us -> 524 us
    psum x1 -> x2, waiting for transfers between devices: 158 us -> 524 us  [supply_the_slots(): return lax.psum(lax.psum(unit, axis_name=group_axis), bus_axis)]
  transfers between devices with their start and end apart: 4 -> 5, of which waited for: 1 -> 2; matrix products, arithmetic and copies ran while one was open for 41% -> 30% of each run, Pallas kernels for 0% -> 0%
where the time goes in v1:
time: 1310 us; the launch traced here: 1290 us
  waiting for transfers between devices  524 us (40%)
  matrix products  453 us (35%)
  local copies, waits for them, and re-layouts  204 us (16%)
  other arithmetic  76.5 us (6%)
  between operations  15.1 us (1%)
  blocking collectives  13.8 us (1%)
    psum x2, waiting for transfers between devices, supply_the_slots(): return lax.psum(lax.psum(unit, axis_name=group_axis), bus_axis)  524 us
    dot_general x224, matrix products, product(): jnp.einsum(pattern, left_side, right_side, preferred_element_type=jnp.flo...  413 us
    while x9, local copies, waits for them, and re-layouts, heads_map(): lax.map(lambda members: function(*members, pieces, scaling), transposed)  35.9 us
    while x32, local copies, waits for them, and re-layouts  31 us
    convert_element_type x6, local copies, waits for them, and re-layouts, sparse_rows(): dense.astype(jnp.float32)  30.7 us
  transfers between devices with their start and end apart: 5, of which 2 were waited for; matrix products, arithmetic and copies ran while one was open for 30% of the time, Pallas kernels for 0%

profile of v1, /device:TPU:1, one launch (start us, length us, event | category | flops | bytes accessed | tf_op | source)
XLA Modules:
  0.0 1294.0 jit_solution(15999842829668564605)
XLA Ops:
  16.9 13.8 %all_to_all.14 = s32[8,1,128]{2,1,0:T(1,128)S(1)} all-to-all(s32[8,1,128]{2,1,0:T(1,128)S(1)} %bitcast.386), channel_id=1, replica_groups=mesh['seq'=8,'rep'=16] {'seq'}, dimensions={0} | all-to-all | bytes 8192 | tf_op jit(solution)/shard_map/all_to_all | solution.py:143
  47.3 4.8 copy.100
  55.2 7.8 reshape.434
  65.1 6.4 scatter_custom_fusion
  76.8 7.8 reshape.431
  90.0 7.8 reshape.432
  105.2 7.8 reshape.433
  113.0 14.1 %select_reduce_fusion = (bf16[64,16,48]{2,1,0:T(8,128)(2,1)S(1)}, bf16[64,16,48]{2,1,0:T(8,128)(2,1)}, bf16[64,16,48]{2,1,0:T(8,128)(2,1)}, bf16[64,16,48]{2,1,0:T(8,128)(2,1)}) fusion(f32[64,16,16,48]{3,2,1,0:T(8,128)} %reshape.434, pred[16,16]{1,0:T(8,128)(4,1)} %copy-done.23, f32[64,16,16,48]{3,2,1,0:T(8,128)} %reshape.432, ...), kind=kLoop, calls=%fused_computation.133 | loop fusion | flops 6094848 | bytes 12976384 | tf_op jit(solution)/shard_map/reduce_sum | solution.py:46
  144.3 142.8 %while.56 = (s32[]{:T(128)}, f32[16,1024,48]{1,2,0:T(8,128)}, f32[16,1024]{1,0:T(8,128)S(1)}, f32[16,1024]{1,0:T(8,128)S(1)}, pred[16,1024]{1,0:T(8,128)(4,1)S(1...) while((s32[]{:T(128)}, f32[16,1024,48]{1,2,0:T(8,128)}, ...), condition=%wide.region_5.6_spmd, body=%wide.region_2.5_spmd.sunk | while | flops 212858880 | bytes 30383244 | solution.py:110
  287.2 7.9 copy.83
  301.4 42.2 %while.57 = (s32[]{:T(128)}, f32[16,64,48]{1,2,0:T(8,128)S(1)}, f32[16,64]{1,0:T(8,128)S(1)}, f32[16,64]{1,0:T(8,128)S(1)}, pred[16,512]{1,0:T(8,128)(4,1)S(1)},...) while((s32[]{:T(128)}, f32[16,64,48]{1,2,0:T(8,128)S(1)}, ...), condition=%wide.region_12.13_spmd, body=%wide.region_9.12_spmd.sunk | while | flops 6520706 | bytes 702321 | solution.py:110
  346.3 13.4 %multiply_convert_fusion.1 = (bf16[1024,16,48]{2,1,0:T(8,128)(2,1)}, f32[1024,16,48]{2,1,0:T(8,128)S(1)}) fusion(f32[1024]{0:T(1024)S(1)} %copy-done.25, f32[1024,16]{1,0:T(8,128)} %copy.97, f32[1024,16]{1,0:T(8,128)S(1)} %copy.96, f32[64,16,48]{2,1,0:T(8,128)S(1)} %copy.95, pred[1024,16]{1,0:T(8,128)(4,1)S(1)} %copy.94, f32[1024,16]{1,0:T(8,128)S(1)} %copy.93, ...), kind=kLoop, calls=%fused_computation.135 | loop fusion | flops 5505024 | bytes 8278016 | tf_op jit(solution)/shard_map/convert_element_type | solution.py:180
  363.1 103.9 %while.59 = (s32[]{:T(128)}, f32[16,64,48]{1,2,0:T(8,128)S(1)}, f32[16,512,48]{1,2,0:T(8,128)}, f32[16,512,48]{1,2,0:T(8,128)}, pred[16,512]{1,0:T(8,128)(4,1)S(...) while((s32[]{:T(128)}, f32[16,64,48]{1,2,0:T(8,128)S(1)}, ...), condition=%wide.region_20.21_spmd, body=%wide.region_19.20_spmd.sunk | while | flops 15985666 | bytes 1278077 | solution.py:110
  481.1 181.1 %while.58 = (s32[]{:T(128)}, f32[16,1024,48]{1,2,0:T(8,128)}, f32[16,1024,48]{1,2,0:T(8,128)}, f32[16,1024,48]{1,2,0:T(8,128)}, pred[16,1024]{1,0:T(8,128)(4,1)S...) while((s32[]{:T(128)}, f32[16,1024,48]{1,2,0:T(8,128)}, ...), condition=%wide.region_15.16_spmd, body=%wide.region_14.15_spmd.sunk | while | flops 513900544 | bytes 21337212 | solution.py:110
  662.5 7.9 copy.102
  670.4 7.8 copy.112
  678.2 7.9 copy.115
  686.1 5.5 copy.98
  699.3 15.1 %fusion.110 = (bf16[1024,16,48]{2,1,0:T(8,128)(2,1)}, bf16[1024,16,48]{2,1,0:T(8,128)(2,1)}, bf16[1024,16,48]{2,1,0:T(8,128)(2,1)}) fusion(f32[16,1024,48]{2,0,1:T(8,128)} %copy.102, f32[64,16,48]{2,1,0:T(8,128)S(1)} %copy.110, pred[1024,16]{1,0:T(8,128)(4,1)} %copy-done.14, f32[64,16,48]{2,1,0:T(8,128)S(1)} %copy.113, f32[16,1024,48]{2,0,1:T(8,128)} %copy.112, ...), kind=kLoop, calls=%fused_computation.127 | loop fusion | flops 7077888 | bytes 14761984 | tf_op jit(solution)/shard_map/convert_element_type | solution.py:221
  714.5 5.5 copy.111
  724.2 5.5 copy.114
  742.8 387.0 %all-reduce.7.cloned.1.call-done = (f32[768,768]{1,0:T(8,128)}, f32[768,768]{1,0:T(8,128)}, f32[768,768]{1,0:T(8,128)}, f32[768,768]{1,0:T(8,128)}) async-done(((f32[768,768]{1,0:T(8,128)}, f32[768,768]{1,0:T(8,128)}, f32[768,768]{1,0:T(8,128)}, f32[768,768]{1,0:T(8,128)}), (f32[768,768]{1,0:T(8,128)}, f32[768,768]{1,0:T(8,128)}, f32[768,768]{1,0:T(8,128)}, ...) | async-done | bytes 9437200 | tf_op jit(solution)/shard_map/psum | solution.py:14
  1129.8 5.0 fusion.117
  1140.7 136.7 %all-reduce.5.cloned.1.call-done = (f32[768,768]{1,0:T(8,128)}, f32[768,768]{1,0:T(8,128)}, f32[768,768]{1,0:T(8,128)}, f32[768,768]{1,0:T(8,128)}) async-done(((f32[768,768]{1,0:T(8,128)}, f32[768,768]{1,0:T(8,128)}, f32[768,768]{1,0:T(8,128)}, f32[768,768]{1,0:T(8,128)}), (f32[768,768]{1,0:T(8,128)}, f32[768,768]{1,0:T(8,128)}, f32[768,768]{1,0:T(8,128)}, ...) | async-done | bytes 9437200 | tf_op jit(solution)/shard_map/psum | solution.py:14
  (608 shorter events, 601.1 us)
Async XLA Ops:
  7.2 23.6 %copy-start = (bf16[1,1024,768]{2,1,0:T(8,128)(2,1)S(1)}, bf16[1,1024,768]{2,1,0:T(8,128)(2,1)}, u32[]{:S(2)}) copy-start(bf16[1,1024,768]{2,1,0:T(8,128)(2,1)} %param.16) | copy-start | bytes 4718596
  36.1 6.4 copy-start.8
  36.1 29.0 %all-to-all-start.1 = ((bf16[8,128,768]{2,1,0:T(8,128)(2,1)}), bf16[8,128,768]{2,1,0:T(8,128)(2,1)}, u32[]{:S(2)}, u32[]{:S(2)}) async-start(bf16[8,128,768]{2,1,0:T(8,128)(2,1)} %broadcast_select_fusion), calls=%async_computation.1 | async-start | bytes 3145728 | tf_op jit(solution)/shard_map/all_to_all | solution.py:145
  40.5 255.2 %all-gather.2.cloned.1.call-start = ((), (), s32[]{:S(2)}) async-start(), calls=%async_computation.3 | async-start | bytes 1769472 | tf_op jit(solution)/shard_map/all_gather | solution.py:22
  64.4 281.9 %copy-start.14 = (pred[1024,16]{1,0:T(8,128)(4,1)}, pred[1024,16]{1,0:T(8,128)(4,1)S(1)}, u32[]{:S(2)}) copy-start(pred[1024,16]{1,0:T(8,128)(4,1)S(1)} %copy.94) | copy-start | bytes 49156
  71.5 3.3 copy-start.10
  132.4 563.3 %reduce-scatter.4.cloned.1.call-start = ((), (), s32[]{:S(2)}) async-start(), calls=%async_computation.4 | async-start | bytes 3538944
  135.9 3.2 copy-start.4
  139.0 3.2 copy-start.28
  139.0 5.2 copy-start.19
  139.0 5.2 copy-start.20
  144.3 142.8 %copy-start.16 = (bf16[64,16,48]{2,1,0:T(8,128)(2,1)S(1)}, bf16[64,16,48]{2,1,0:T(8,128)(2,1)}, u32[]{:S(2)}) copy-start(bf16[64,16,48]{2,1,0:T(8,128)(2,1)} %get-tuple-element.310) | copy-start | bytes 294916
  343.6 2.7 copy-start.25
  346.3 13.4 %copy-start.3 = (bf16[1024,16,48]{2,1,0:T(8,128)(2,1)S(1)}, bf16[1024,16,48]{2,1,0:T(8,128)(2,1)}, u32[]{:S(2)}) copy-start(bf16[1024,16,48]{2,1,0:T(8,128)(2,1)} %copy.100) | copy-start | bytes 4718596
  359.7 3.0 copy-start.22
  474.8 655.0 %all-reduce.7.cloned.1.call-start = ((), (), s32[]{:S(2)}) async-start(), calls=%async_computation.6 | async-start | bytes 18874368 | tf_op jit(solution)/shard_map/psum | solution.py:14
  686.1 5.5 copy-start.9
  714.5 5.5 copy-start.11
  742.7 534.7 %all-reduce.5.cloned.1.call-start = ((), (), s32[]{:S(2)}) async-start(), calls=%async_computation.5 | async-start | bytes 18874368 | tf_op jit(solution)/shard_map/psum | solution.py:14
  1129.8 5.0 copy-start.12
  1129.8 5.0 copy-start.29
  1277.4 3.4 copy-start.7
  1280.8 2.5 copy-start.6
  1283.3 3.9 copy-start.1
  (27 other events, 49.5 us)
Sparse Core Ops, SparseCore 0:
  132.6 52.8 all-gather.1
  474.9 81.6 reduce-scatter.3
  742.8 386.9 all-reduce.6
  1132.4 144.9 all-reduce.4
